TPU v7x, 128 devices: a whole 4x4x4 slice. The times are simulated.
128 devices in a mesh: az: 32 (over z, y_lo, x), rad: 4 (over y_hi, core).
Axes of the slice: x: 4, y: 4 (y_hi: 2, y_lo: 2; y = y_hi * 2 + y_lo), z: 4, core: 2. Of those that a mesh axis runs over, the one named last changes fastest.
Arguments:
- state: bfloat16 [4, 64, 2048, 512], P(None, None, 'az', 'rad'), may hold values from -6 to 6
- source: bfloat16 [64, 2048, 512], P(None, 'az', 'rad'), may hold values from -6 to 6
- shear: bfloat16 [64, 2048, 512], P(None, 'az', 'rad'), may hold values from 0.5 to 4
- permeability: bfloat16 [64, 2048, 512], P(None, 'az', 'rad'), may hold values from 0.099609375 to 10
- radial_basis: float32 [512, 512], P('rad'), may hold values from -1 to 2
- radial_eigen: float32 [512], replicated, may hold values from 4e-05 to 4
Outputs:
- correction: bfloat16 [4, 64, 2048, 512], P(None, None, 'az', 'rad')
All inputs are finite; a program needn't handle non-finite values.
Results may differ from a plain program's by a relative error of at most 0.001.
Values may be sent and summed in bfloat16 or wider, within the bound.
A program may use at most 192 MiB of HBM per device.

v0:
```python
import math
import jax
import jax.numpy as jnp
from jax import lax
from jax.sharding import PartitionSpec as P

NH = 64
biot_coupling = 2.0
storage = 1.0


def padded_2(cells, sides, width):
    for axis, dim in sides:
        count = lax.axis_size(axis)
        head = lax.slice_in_dim(cells, 0, width, axis=dim)
        tail = lax.slice_in_dim(cells, cells.shape[dim] - width, cells.shape[dim], axis=dim)
        cells = jnp.concatenate(
            [
                lax.ppermute(tail, axis, [(i, (i + 1) % count) for i in range(count)]),
                cells,
                lax.ppermute(head, axis, [((i + 1) % count, i) for i in range(count)]),
            ],
            axis=dim,
        )
    return cells


def contract(form, left, right):
    return jnp.einsum(
        form, left, right, precision=lax.Precision.HIGHEST, preferred_element_type=jnp.float32
    )


def neighbor(extended, grid_axis, offset):
    lead = extended.ndim - 3
    window = [slice(None)] * lead + [slice(1, -1)] * 3
    length = extended.shape[lead + grid_axis]
    window[lead + grid_axis] = slice(1 + offset, length - 1 + offset)
    return extended[tuple(window)]


def stencil(extended, source_block):
    center = neighbor(extended, 0, 0)
    diagonal = jnp.zeros_like(center[4])
    momentum = [jnp.zeros_like(center[0]), jnp.zeros_like(center[0]), jnp.zeros_like(center[0])]
    fluid = jnp.zeros_like(center[0])
    for grid_axis in (0, 1, 2):
        for offset in (1, -1):
            beside = neighbor(extended, grid_axis, offset)
            shear_face = 0.5 * (center[4] + beside[4])
            flow_face = 0.5 * (center[5] + beside[5])
            diagonal = diagonal + shear_face
            momentum = [
                momentum[channel] + shear_face * (center[channel] - beside[channel])
                for channel in range(3)
            ]
            fluid = fluid + flow_face * (center[3] - beside[3])
    component_axes = (2, 1, 0)
    pressure = extended[3]
    spread = jnp.zeros_like(center[0])
    parts = []
    for channel in range(3):
        grid_axis = component_axes[channel]
        gradient = 0.5 * (neighbor(pressure, grid_axis, 1) - neighbor(pressure, grid_axis, -1))
        parts.append(-(momentum[channel] + biot_coupling * gradient))
        member = extended[channel]
        spread = spread + 0.5 * (neighbor(member, grid_axis, 1) - neighbor(member, grid_axis, -1))
    parts.append(source_block + biot_coupling * spread + storage * center[3] + fluid)
    return (jnp.stack(parts), diagonal)


def cosine_table(extent):
    row_ids = jnp.arange(extent, dtype=jnp.float32)[:, None]
    col_ids = jnp.arange(extent, dtype=jnp.float32)[None, :]
    scaled = jnp.where(row_ids == 0, math.sqrt(1.0 / extent), math.sqrt(2.0 / extent))
    return scaled * jnp.cos(math.pi * (col_ids + 0.5) * row_ids / extent)


def fourier_pair(rows_len, cols_len, period):
    row_ids = jnp.arange(rows_len, dtype=jnp.int32)[:, None]
    col_ids = jnp.arange(cols_len, dtype=jnp.int32)[None, :]
    angle = 2.0 * math.pi / period * (row_ids * col_ids % period).astype(jnp.float32)
    return (jnp.cos(angle), jnp.sin(angle))


def spectral_solve(coeffs, mode_start, radial_eigen):
    moved = lax.all_to_all(coeffs, "az", split_axis=0, concat_axis=2, tiled=True)
    mode_count, level_count, length = moved.shape
    inner_len = 128
    outer_len = length // inner_len
    lines = moved.reshape(mode_count, level_count, outer_len, inner_len)
    cos_outer, sin_outer = fourier_pair(outer_len, outer_len, outer_len)
    cos_inner, sin_inner = fourier_pair(inner_len, inner_len, inner_len)
    tw_cos, tw_sin = fourier_pair(outer_len, inner_len, length)
    real_one = contract("mlab,ak->mlkb", lines, cos_outer)
    imag_one = -contract("mlab,ak->mlkb", lines, sin_outer)
    turned_real = real_one * tw_cos + imag_one * tw_sin
    turned_imag = imag_one * tw_cos - real_one * tw_sin
    spec_real = contract("mlkb,bj->mlkj", turned_real, cos_inner) + contract(
        "mlkb,bj->mlkj", turned_imag, sin_inner
    )
    spec_imag = contract("mlkb,bj->mlkj", turned_imag, cos_inner) - contract(
        "mlkb,bj->mlkj", turned_real, sin_inner
    )
    mode_eigen = lax.dynamic_slice_in_dim(radial_eigen, mode_start, mode_count)
    levels = jnp.arange(level_count, dtype=jnp.int32).astype(jnp.float32)
    height_eigen = 4.0 * jnp.sin(math.pi * levels / (2.0 * NH)) ** 2
    first_ids = jnp.arange(outer_len, dtype=jnp.float32)[:, None]
    second_ids = jnp.arange(inner_len, dtype=jnp.float32)[None, :]
    waves = first_ids + outer_len * second_ids
    azimuth_eigen = 4.0 * jnp.sin(math.pi * waves / length) ** 2
    totals = (
        storage
        + mode_eigen[:, None, None, None]
        + height_eigen[None, :, None, None]
        + azimuth_eigen[None, None, :, :]
    )
    solved_real = spec_real / totals
    solved_imag = spec_imag / totals
    back_real = contract("mlkj,bj->mlkb", solved_real, cos_inner) - contract(
        "mlkj,bj->mlkb", solved_imag, sin_inner
    )
    back_imag = contract("mlkj,bj->mlkb", solved_imag, cos_inner) + contract(
        "mlkj,bj->mlkb", solved_real, sin_inner
    )
    untwist_real = back_real * tw_cos - back_imag * tw_sin
    untwist_imag = back_imag * tw_cos + back_real * tw_sin
    signal = contract("mlkb,ak->mlab", untwist_real, cos_outer) - contract(
        "mlkb,ak->mlab", untwist_imag, sin_outer
    )
    signal = (signal * (1.0 / length)).reshape(mode_count, level_count, length)
    return lax.all_to_all(signal, "az", split_axis=2, concat_axis=0, tiled=True)


def precondition(residual_p, radial_basis, radial_eigen):
    cosine = cosine_table(NH)
    heights = contract("lh,har->lar", cosine, residual_p)
    local_radii = heights.shape[2]
    columns = radial_basis
    coeffs = lax.psum_scatter(
        contract("lar,rm->mla", heights, columns), "rad", scatter_dimension=0, tiled=True
    )
    mode_start = lax.axis_index("rad") * local_radii + lax.axis_index("az") * (
        local_radii // lax.axis_size("az")
    )
    solved = spectral_solve(coeffs, mode_start, radial_eigen)
    columns = radial_basis
    planes = contract("mla,rm->lar", lax.all_gather(solved, "rad", axis=0, tiled=True), columns)
    return contract("lh,lar->har", cosine, planes)


def body(state, source, shear, permeability, radial_basis, radial_eigen):
    stacked = jnp.concatenate([state, shear[None], permeability[None]], axis=0)
    padded = padded_2(stacked, (("az", 2), ("rad", 3)), 1)
    rad_count = lax.axis_size("rad")
    rad_place = lax.axis_index("rad")
    column = lax.broadcasted_iota(jnp.int32, (padded.shape[3],), 0)
    outside = (column == 0) & (rad_place == 0) | (column == padded.shape[3] - 1) & (
        rad_place == rad_count - 1
    )
    padded = jnp.where(outside, jnp.zeros((), padded.dtype), padded)
    extended = jnp.pad(padded.astype(jnp.float32), ((0, 0), (1, 1), (0, 0), (0, 0)))
    residual, diagonal = stencil(extended, source.astype(jnp.float32))
    moment_step = residual[:3] / diagonal
    press_step = precondition(residual[3], radial_basis, radial_eigen)
    local_rr = jnp.sum(residual * residual)
    local_rz = jnp.sum(residual[:3] * moment_step) + jnp.sum(residual[3] * press_step)
    total_rr, total_rz = lax.psum((local_rr, local_rz), ("az", "rad"))
    alpha = total_rr / total_rz
    return jnp.concatenate(
        [
            (alpha * moment_step).astype(jnp.bfloat16),
            (alpha * press_step).astype(jnp.bfloat16)[None],
        ],
        axis=0,
    )


def solution(mesh):
    placed = (
        P(None, None, "az", "rad"),
        P(None, "az", "rad"),
        P(None, "az", "rad"),
        P(None, "az", "rad"),
        P("rad", None),
        P(),
    )
    return jax.shard_map(
        body, mesh=mesh, in_specs=placed, out_specs=P(None, None, "az", "rad"), check_vma=False
    )
```

profile of v0, /device:TPU:1, one launch (start us, length us, event | category | flops | bytes accessed | tf_op | source)
XLA Modules:
  0.0 562.8 jit_solution(13840592234167820502)
XLA Ops:
  13.7 7.9 %collective-permute-start.1 = (bf16[6,64,1,128]{3,1,2,0:T(8,128)(2,1)S(1)}, bf16[6,64,1,128]{3,1,2,0:T(8,128)(2,1)S(1)}, u32[]{:S(2)}, u32[]{:S(2)}) collective-permute-start(bf16[6,64,1,128]{3,1,2,0:T(8,128)(2,1)S(1)} %get-tuple-element.21), channel_id=1, source_target_pairs={{4,0},{8,4},{12,8},{16,12},{20,16},{24,20},{28,24},{32,28},{36,32}... | collective-permute-start | bytes 294920 | tf_op jit(solution)/shard_map/ppermute | solution.py:21
  23.2 6.0 %collective-permute-done = bf16[6,64,1,128]{3,1,2,0:T(8,128)(2,1)S(1)} collective-permute-done((bf16[6,64,1,128]{3,1,2,0:T(8,128)(2,1)S(1)}, bf16[6,64,1,128]{3,1,2,0:T(8,128)(2,1)S(1)}, u32[]{:S(2)}, u32[]{:S(2)}) %collective-permute-start) | collective-permute-done | bytes 98336 | tf_op jit(solution)/shard_map/ppermute | solution.py:19
  33.1 6.4 %fusion.237 = (bf16[6,64,66,1]{3,1,2,0:T(8,128)(2,1)}, bf16[6,64,66,1]{3,1,2,0:T(8,128)(2,1)}) fusion(bf16[6,64,66,128]{3,1,2,0:T(8,128)(2,1)S(1)} %pad_maximum_fusion), kind=kLoop, calls=%fused_computation.305 | loop fusion | bytes 202752 | tf_op jit(solution)/shard_map/slice | solution.py:16
  39.5 8.5 %copy.41 = bf16[6,64,66,1]{2,1,3,0:T(8,128)(2,1)S(1)} copy(bf16[6,64,66,1]{3,1,2,0:T(8,128)(2,1)} %get-tuple-element.19) | data formatting | bytes 101376 | tf_op jit(solution)/shard_map/slice | solution.py:15
  50.1 8.5 %copy.40 = bf16[6,64,66,1]{2,1,3,0:T(8,128)(2,1)S(1)} copy(bf16[6,64,66,1]{3,1,2,0:T(8,128)(2,1)} %get-tuple-element.18) | data formatting | bytes 101376 | tf_op jit(solution)/shard_map/slice | solution.py:16
  61.4 11.4 %copy.43 = bf16[6,64,66,1]{3,1,2,0:T(8,128)(2,1)} copy(bf16[6,64,66,1]{2,1,3,0:T(8,128)(2,1)S(1)} %collective-permute-done.3) | data formatting | bytes 101376 | tf_op jit(solution)/shard_map/ppermute | solution.py:21
  72.8 11.4 %copy.42 = bf16[6,64,66,1]{3,1,2,0:T(8,128)(2,1)} copy(bf16[6,64,66,1]{2,1,3,0:T(8,128)(2,1)S(1)} %collective-permute-done.2) | data formatting | bytes 101376 | tf_op jit(solution)/shard_map/ppermute | solution.py:19
  84.2 22.1 %fusion = f32[6,64,66,130]{3,1,2,0:T(8,128)} fusion(bf16[6,64,66,1]{3,1,2,0:T(8,128)(2,1)} %copy.43, bf16[6,64,1,128]{3,1,2,0:T(8,128)(2,1)S(1)} %collective-permute-done.1, bf16[1,64,64,128]{3,1,2,0:T(8,128)(2,1)S(1)} %get-tuple-element.24, bf16[1,64,64,128]{3,1,2,0:T(8,128)(2,1)S(1)} %get-tuple-element.25, bf16[4,64,64,128]{3,1,2,0:T(8,128)(2,1)} %copy-done.1, ...), kind=kLoop, calls=%fused_computation.17 | loop fusion | flops 52715520 | bytes 19768450 | tf_op jit(solution)/shard_map/convert_element_type | solution.py:162
  106.3 10.0 %fusion.2 = (f32[66,66,130]{2,0,1:T(8,128)}, f32[66,66,130]{2,0,1:T(8,128)S(1)}, f32[66,66,130]{2,0,1:T(8,128)S(1)}, f32[66,66,130]{2,0,1:T(8,128)}) fusion(f32[6,64,66,130]{3,1,2,0:T(8,128)} %fusion), kind=kLoop, calls=%fused_computation.24 | loop fusion | bytes 22239360 | tf_op jit(solution)/shard_map/squeeze | solution.py:59
  116.3 28.8 %fusion.45 = f32[64,64,128]{2,0,1:T(8,128)S(1)} fusion(f32[6,64,66,130]{3,1,2,0:T(8,128)} %fusion, f32[66,66,130]{2,0,1:T(8,128)S(1)} %get-tuple-element.16, f32[66,66,130]{2,0,1:T(8,128)S(1)} %get-tuple-element.15, f32[66,66,130]{2,0,1:T(8,128)} %get-tuple-element.17, bf16[64,64,128]{2,1,0:T(8,128)(2,1)S(1)} %copy-done.10), kind=kLoop, calls=%fused_computation.71 | loop fusion | flops 19922944 | bytes 62652416 | tf_op jit(solution)/shard_map/add | solution.py:68
  147.2 9.4 %convolution_bitcast_fusion = f32[512,64,64]{0,2,1:T(8,128)} fusion(f32[64,64,128]{2,0,1:T(8,128)S(1)} %fusion.139, f32[128,512]{1,0:T(8,128)S(1)} %copy-done), kind=kOutput, calls=%fused_computation.29 | convolution fusion | flops 3221225472 | bytes 10747904 | tf_op jit(solution)/shard_map/lar,rm->mla/dot_general | solution.py:29
  156.6 73.1 %reduce-scatter.2.cloned.1.call-done = f32[128,64,64]{0,2,1:T(8,128)} async-done(((f32[512,64,64]{0,2,1:T(8,128)}), f32[128,64,64]{0,2,1:T(8,128)}) %reduce-scatter.2.cloned.1.call-update) | async-done | bytes 2097168 | tf_op jit(solution)/shard_map/reduce_scatter | solution.py:140
  240.7 7.0 %all-to-all-start = ((f32[32,1,16384]{2,1,0:T(1,128)}), f32[32,1,16384]{2,1,0:T(1,128)S(1)}, u32[]{:S(2)}, u32[]{:S(2)}) async-start(f32[32,1,16384]{2,1,0:T(1,128)} %reshape.226), calls=%async_computation.1 | async-start | bytes 4194304 | tf_op jit(solution)/shard_map/all_to_all | solution.py:87
  248.9 26.2 %all-to-all-done = f32[32,1,16384]{2,1,0:T(1,128)S(1)} async-done(((f32[32,1,16384]{2,1,0:T(1,128)}), f32[32,1,16384]{2,1,0:T(1,128)S(1)}, u32[]{:S(2)}, u32[]{:S(2)}) %all-to-all-start) | async-done | bytes 2097184 | tf_op jit(solution)/shard_map/all_to_all | solution.py:87
  277.0 7.4 %reduce = f32[32,16384]{1,0:T(8,128)S(1)} reduce(f32[32,1,16384]{2,1,0:T(1,128)} %copy-done.8, f32[]{:T(128)} %broadcast.258), dimensions={1}, to_apply=%all_to_all.24.reduce_sub_computation | reduce | bytes 4194308 | tf_op jit(solution)/shard_map/all_to_all | solution.py:87
  287.4 6.7 %copy.48 = f32[4,64,32,64]{3,2,1,0:T(8,128)} copy(f32[4,64,32,64]{3,1,0,2:T(8,128)} %bitcast.206) | data formatting | bytes 4194304 | tf_op jit(solution)/shard_map/all_to_all | solution.py:87
  331.7 32.7 %all_to_all.33 = f32[32,1,16384]{2,1,0:T(1,128)} all-to-all(f32[32,1,16384]{2,1,0:T(1,128)S(1)} %reshape.228), channel_id=1, replica_groups=mesh['az'=32,'rad'=4] {'az'}, dimensions={0} | all-to-all | bytes 4194304 | tf_op jit(solution)/shard_map/all_to_all | solution.py:132
  364.4 7.4 %reduce.1 = f32[32,16384]{1,0:T(8,128)S(1)} reduce(f32[32,1,16384]{2,1,0:T(1,128)} %all_to_all.33, f32[]{:T(128)} %broadcast.258), dimensions={1}, to_apply=%all_to_all.27.reduce_sub_computation | reduce | bytes 4194308 | tf_op jit(solution)/shard_map/all_to_all | solution.py:132
  386.6 16.3 %multiply_bitcast_fusion.1 = (f32[64,64,128]{2,0,1:T(8,128)}, f32[1,64,64,128]{3,1,2,0:T(8,128)}, f32[1,64,64,128]{3,1,2,0:T(8,128)}, f32[1,64,64,128]{3,1,2,0:T...) fusion(f32[6,64,66,130]{3,1,2,0:T(8,128)} %fusion), kind=kLoop, calls=%fused_computation.171 | loop fusion | flops 6291456 | bytes 51118080 | tf_op jit(solution)/shard_map/div | solution.py:164
  402.9 17.2 %fusion.73 = f32[1,64,64,128]{3,1,2,0:T(8,128)} fusion(f32[66,66,130]{2,0,1:T(8,128)S(1)} %bitcast.203, f32[6,64,66,130]{3,1,2,0:T(8,128)} %fusion, f32[1,64,64,128]{3,1,2,0:T(8,128)} %get-tuple-element.13, f32[1,64,64,128]{3,1,2,0:T(8,128)} %get-tuple-element.12, f32[1,64,64,128]{3,1,2,0:T(8,128)} %get-tuple-element.11, ...), kind=kLoop, calls=%fused_computation.112 | loop fusion | flops 13631488 | bytes 55312384 | tf_op jit(solution)/shard_map/stack | solution.py:69
  420.1 19.5 %fusion.80 = f32[1,64,64,128]{3,1,2,0:T(8,128)} fusion(f32[66,66,130]{2,0,1:T(8,128)} %get-tuple-element.14, f32[6,64,66,130]{3,1,2,0:T(8,128)} %fusion, f32[1,64,64,128]{3,1,2,0:T(8,128)} %get-tuple-element.13, f32[1,64,64,128]{3,1,2,0:T(8,128)} %get-tuple-element.12, f32[1,64,64,128]{3,1,2,0:T(8,128)} %get-tuple-element.11, ...), kind=kLoop, calls=%fused_computation.124 | loop fusion | flops 13631488 | bytes 55312384 | tf_op jit(solution)/shard_map/stack | solution.py:69
  439.6 18.4 %fusion.87 = f32[1,64,64,128]{3,1,2,0:T(8,128)} fusion(f32[66,66,130]{2,0,1:T(8,128)} %get-tuple-element.14, f32[6,64,66,130]{3,1,2,0:T(8,128)} %fusion, f32[1,64,64,128]{3,1,2,0:T(8,128)} %get-tuple-element.13, f32[1,64,64,128]{3,1,2,0:T(8,128)} %get-tuple-element.12, f32[1,64,64,128]{3,1,2,0:T(8,128)} %get-tuple-element.11, ...), kind=kLoop, calls=%fused_computation.136 | loop fusion | flops 13631488 | bytes 55312384 | tf_op jit(solution)/shard_map/stack | solution.py:69
  464.8 10.2 %fusion.120 = f32[64,64,128]{2,0,1:T(8,128)S(1)} fusion(f32[512,64,64]{0,1,2:T(8,128)} %all-gather.2.cloned.1.call-done, f32[128,512]{1,0:T(8,128)S(1)} %copy-done), kind=kOutput, calls=%fused_computation.181 | convolution fusion | flops 3221225472 | bytes 10747904 | tf_op jit(solution)/shard_map/mla,rm->lar/dot_general | solution.py:29
  480.1 64.7 %all-reduce.1 = (f32[]{:T(128)}, f32[]{:T(128)}) all-reduce(f32[]{:T(128)} %fusion.1, f32[]{:T(128)S(6)} %add.397), channel_id=1, replica_groups=mesh['az'=32,'rad'=4] {'az','rad'}, use_global_device_ids=true, to_apply=%region_1.2 | all-reduce | flops 2 | bytes 16 | tf_op jit(solution)/shard_map/psum | solution.py:168
  (84 shorter events, 109.3 us)
Async XLA Ops:
  6.5 140.7 %copy-start = (f32[128,512]{1,0:T(8,128)S(1)}, f32[128,512]{1,0:T(8,128)}, u32[]{:S(2)}) copy-start(f32[128,512]{1,0:T(8,128)} %param.10) | copy-start | bytes 786436
  6.5 5.1 copy-start.11
  6.5 223.1 %reduce-scatter.2.cloned.1.call-start = ((), (), s32[]{:S(2)}) async-start(), calls=%async_computation.3 | async-start | bytes 10485760 | tf_op jit(solution)/shard_map/reduce_scatter | solution.py:140
  6.5 5.1 copy-start.12
  11.6 2.0 copy-start.1
  13.7 9.5 %collective-permute-start.1 = (bf16[6,64,1,128]{3,1,2,0:T(8,128)(2,1)S(1)}, bf16[6,64,1,128]{3,1,2,0:T(8,128)(2,1)S(1)}, u32[]{:S(2)}, u32[]{:S(2)}) collective-permute-start(bf16[6,64,1,128]{3,1,2,0:T(8,128)(2,1)S(1)} %get-tuple-element.21), channel_id=1, source_target_pairs={{4,0},{8,4},{12,8},{16,12},{20,16},{24,20},{28,24},{32,28},{36,32}... | collective-permute-start | bytes 294920 | tf_op jit(solution)/shard_map/ppermute | solution.py:21
  21.5 7.7 %collective-permute-start = (bf16[6,64,1,128]{3,1,2,0:T(8,128)(2,1)S(1)}, bf16[6,64,1,128]{3,1,2,0:T(8,128)(2,1)S(1)}, u32[]{:S(2)}, u32[]{:S(2)}) collective-permute-start(bf16[6,64,1,128]{3,1,2,0:T(8,128)(2,1)S(1)} %get-tuple-element.20), channel_id=1, source_target_pairs={{0,4},{4,8},{8,12},{12,16},{16,20},{20,24},{24,28},{28,32},{32,36}... | collective-permute-start | bytes 294920 | tf_op jit(solution)/shard_map/ppermute | solution.py:19
  47.9 13.4 %collective-permute-start.3 = (bf16[6,64,66,1]{2,1,3,0:T(8,128)(2,1)S(1)}, bf16[6,64,66,1]{2,1,3,0:T(8,128)(2,1)S(1)}, u32[]{:S(2)}, u32[]{:S(2)}) collective-permute-start(bf16[6,64,66,1]{2,1,3,0:T(8,128)(2,1)S(1)} %copy.41), channel_id=1, source_target_pairs={{1,0},{2,1},{3,2},{0,3},{5,4},{6,5},{7,6},{4,7},{9,8},{10,9},{11,1... | collective-permute-start | bytes 152072 | tf_op jit(solution)/shard_map/ppermute | solution.py:21
  58.6 14.2 %collective-permute-start.2 = (bf16[6,64,66,1]{2,1,3,0:T(8,128)(2,1)S(1)}, bf16[6,64,66,1]{2,1,3,0:T(8,128)(2,1)S(1)}, u32[]{:S(2)}, u32[]{:S(2)}) collective-permute-start(bf16[6,64,66,1]{2,1,3,0:T(8,128)(2,1)S(1)} %copy.40), channel_id=1, source_target_pairs={{0,1},{1,2},{2,3},{3,0},{4,5},{5,6},{6,7},{7,4},{8,9},{9,10},{10,1... | collective-permute-start | bytes 152072 | tf_op jit(solution)/shard_map/ppermute | solution.py:19
  106.3 10.0 %copy-start.10 = (bf16[64,64,128]{2,1,0:T(8,128)(2,1)S(1)}, bf16[64,64,128]{2,1,0:T(8,128)(2,1)}, u32[]{:S(2)}) copy-start(bf16[64,64,128]{2,1,0:T(8,128)(2,1)} %param.7) | copy-start | bytes 3145732
  145.1 2.1 copy-start.2
  240.7 34.5 %all-to-all-start = ((f32[32,1,16384]{2,1,0:T(1,128)}), f32[32,1,16384]{2,1,0:T(1,128)S(1)}, u32[]{:S(2)}, u32[]{:S(2)}) async-start(f32[32,1,16384]{2,1,0:T(1,128)} %reshape.226), calls=%async_computation.1 | async-start | bytes 4194304 | tf_op jit(solution)/shard_map/all_to_all | solution.py:87
  247.6 217.1 %all-gather.2.cloned.1.call-start = ((), (), s32[]{:S(2)}) async-start(), calls=%async_computation.4 | async-start | bytes 10485760 | tf_op jit(solution)/shard_map/all_gather | solution.py:148
  275.1 1.3 copy-start.8
  386.5 16.3 %slice-start = ((s8[4866048]{0:T(1024)(128)(4,1)}), s8[671744]{0:T(1024)(128)(4,1)S(1)}, s32[]{:S(2)}) async-start(s8[4866048]{0:T(1024)(128)(4,1)} %bitcast.202), calls=%async_computation.5 | async-start | bytes 1343488
  386.6 16.3 %slice-start.1 = ((s8[4866048]{0:T(1024)(128)(4,1)}), s8[4194304]{0:T(1024)(128)(4,1)S(1)}, s32[]{:S(2)}) async-start(s8[4866048]{0:T(1024)(128)(4,1)} %bitcast.202), calls=%async_computation.6 | async-start | bytes 8388608
  439.6 18.4 %copy-start.3 = (f32[64,64,128]{2,0,1:T(8,128)S(1)}, f32[64,64,128]{2,0,1:T(8,128)}, u32[]{:S(2)}) copy-start(f32[64,64,128]{2,0,1:T(8,128)} %copy-done.2) | copy-start | bytes 6291460
  439.6 18.4 %copy-start.4 = (f32[1,64,64,128]{3,1,2,0:T(8,128)S(1)}, f32[1,64,64,128]{3,1,2,0:T(8,128)}, u32[]{:S(2)}) copy-start(f32[1,64,64,128]{3,1,2,0:T(8,128)} %fusion.73) | copy-start | bytes 6291460
  458.0 4.5 copy-start.5
  458.0 4.5 copy-start.6
  458.0 4.5 copy-start.7
  546.0 4.2 copy-start.9
Sparse Core Ops, SparseCore 0:
  156.7 72.8 reduce-scatter.1
  386.7 64.0 all-gather.1
where the time goes:
time: 571 us; the launch traced here: 563 us
  other arithmetic  153 us (27%)
  local copies, waits for them, and re-layouts  117 us (20%)
  waiting for transfers between devices  107 us (19%)
  blocking collectives  97.4 us (17%)
  matrix products  51.5 us (9%)
  starting transfers between devices  20 us (4%)
  between operations  16.6 us (3%)
    reduce_scatter x1, waiting for transfers between devices, precondition(): lax.psum_scatter(contract('lar,rm->mla', heights, columns), 'rad', scatte...  73.1 us
    psum x1, blocking collectives, body(): total_rr, total_rz = lax.psum((local_rr, local_rz), ('az', 'rad'))  64.7 us
    another operation x3, other arithmetic, stencil(): return (jnp.stack(parts), diagonal)  55 us
    dot_general x16, matrix products, contract(): jnp.einsum(form, left, right, precision=lax.Precision.HIGHEST, preferred_...  51.5 us
    all_to_all x1, blocking collectives, spectral_solve(): return lax.all_to_all(signal, 'az', split_axis=2, concat_axis=0, tiled=True)  32.7 us
    add x1, other arithmetic, stencil(): source_block + biot_coupling * spread + storage * center[3] + fluid  28.8 us
    all_to_all x1, waiting for transfers between devices, spectral_solve(): lax.all_to_all(coeffs, 'az', split_axis=0, concat_axis=2, tiled=True)  26.2 us
    unnamed x35, local copies, waits for them, and re-layouts  25.1 us
  transfers between devices with their start and end apart: 7, of which 4 were waited for; matrix products, arithmetic and copies ran while one was open for 18% of the time, Pallas kernels for 0%

commit v1 on v0

--- a/solution.py
+++ b/solution.py
@@ -165,7 +165,7 @@
     press_step = precondition(residual[3], radial_basis, radial_eigen)
     local_rr = jnp.sum(residual * residual)
     local_rz = jnp.sum(residual[:3] * moment_step) + jnp.sum(residual[3] * press_step)
-    total_rr, total_rz = lax.psum((local_rr, local_rz), ("az", "rad"))
+    total_rr, total_rz = lax.psum(lax.psum((local_rr, local_rz), "az"), "rad")
     alpha = total_rr / total_rz
     return jnp.concatenate(
         [

time: 571 us -> 597 us (1.046)
  blocking collectives: 97.4 us -> 123 us
    psum x1 -> x2, blocking collectives: 64.7 us -> 90.4 us  [body(): total_rr, total_rz = lax.psum(lax.psum((local_rr, local_rz), 'az'), 'rad')]
  transfers between devices with their start and end apart: 7 -> 7, of which waited for: 4 -> 4; matrix products, arithmetic and copies ran while one was open for 18% -> 17% of each run, Pallas kernels for 0% -> 0%
where the time goes in v1:
time: 597 us; the launch traced here: 589 us
  other arithmetic  153 us (26%)
  blocking collectives  123 us (21%)
  local copies, waits for them, and re-layouts  117 us (20%)
  waiting for transfers between devices  107 us (18%)
  matrix products  51.5 us (9%)
  starting transfers between devices  20 us (3%)
  between operations  16.7 us (3%)
    psum x2, blocking collectives, body(): total_rr, total_rz = lax.psum(lax.psum((local_rr, local_rz), 'az'), 'rad')  90.4 us
    reduce_scatter x1, waiting for transfers between devices, precondition(): lax.psum_scatter(contract('lar,rm->mla', heights, columns), 'rad', scatte...  73.1 us
    another operation x3, other arithmetic, stencil(): return (jnp.stack(parts), diagonal)  55.1 us
    dot_general x16, matrix products, contract(): jnp.einsum(form, left, right, precision=lax.Precision.HIGHEST, preferred_...  51.5 us
    all_to_all x1, blocking collectives, spectral_solve(): return lax.all_to_all(signal, 'az', split_axis=2, concat_axis=0, tiled=True)  32.7 us
    add x1, other arithmetic, stencil(): source_block + biot_coupling * spread + storage * center[3] + fluid  28.7 us
    all_to_all x1, waiting for transfers between devices, spectral_solve(): lax.all_to_all(coeffs, 'az', split_axis=0, concat_axis=2, tiled=True)  26.2 us
    unnamed x35, local copies, waits for them, and re-layouts  25.1 us
  transfers between devices with their start and end apart: 7, of which 4 were waited for; matrix products, arithmetic and copies ran while one was open for 17% of the time, Pallas kernels for 0%

profile of v1, /device:TPU:1, one launch (start us, length us, event | category | flops | bytes accessed | tf_op | source)
XLA Modules:
  0.0 588.6 jit_solution(7174092836185913441)
XLA Ops:
  13.7 7.9 %collective-permute-start.1 = (bf16[6,64,1,128]{3,1,2,0:T(8,128)(2,1)S(1)}, bf16[6,64,1,128]{3,1,2,0:T(8,128)(2,1)S(1)}, u32[]{:S(2)}, u32[]{:S(2)}) collective-permute-start(bf16[6,64,1,128]{3,1,2,0:T(8,128)(2,1)S(1)} %get-tuple-element.23), channel_id=1, source_target_pairs={{4,0},{8,4},{12,8},{16,12},{20,16},{24,20},{28,24},{32,28},{36,32}... | collective-permute-start | bytes 294920 | tf_op jit(solution)/shard_map/ppermute | solution.py:21
  33.1 6.3 %fusion.237 = (bf16[6,64,66,1]{3,1,2,0:T(8,128)(2,1)}, bf16[6,64,66,1]{3,1,2,0:T(8,128)(2,1)}) fusion(bf16[6,64,66,128]{3,1,2,0:T(8,128)(2,1)S(1)} %pad_maximum_fusion), kind=kLoop, calls=%fused_computation.305 | loop fusion | bytes 202752 | tf_op jit(solution)/shard_map/slice | solution.py:16
  39.5 8.5 %copy.41 = bf16[6,64,66,1]{2,1,3,0:T(8,128)(2,1)S(1)} copy(bf16[6,64,66,1]{3,1,2,0:T(8,128)(2,1)} %get-tuple-element.21) | data formatting | bytes 101376 | tf_op jit(solution)/shard_map/slice | solution.py:15
  50.1 8.5 %copy.40 = bf16[6,64,66,1]{2,1,3,0:T(8,128)(2,1)S(1)} copy(bf16[6,64,66,1]{3,1,2,0:T(8,128)(2,1)} %get-tuple-element.20) | data formatting | bytes 101376 | tf_op jit(solution)/shard_map/slice | solution.py:16
  61.4 11.4 %copy.43 = bf16[6,64,66,1]{3,1,2,0:T(8,128)(2,1)} copy(bf16[6,64,66,1]{2,1,3,0:T(8,128)(2,1)S(1)} %collective-permute-done.3) | data formatting | bytes 101376 | tf_op jit(solution)/shard_map/ppermute | solution.py:21
  72.8 11.4 %copy.42 = bf16[6,64,66,1]{3,1,2,0:T(8,128)(2,1)} copy(bf16[6,64,66,1]{2,1,3,0:T(8,128)(2,1)S(1)} %collective-permute-done.2) | data formatting | bytes 101376 | tf_op jit(solution)/shard_map/ppermute | solution.py:19
  84.2 22.1 %fusion = f32[6,64,66,130]{3,1,2,0:T(8,128)} fusion(bf16[6,64,66,1]{3,1,2,0:T(8,128)(2,1)} %copy.43, bf16[6,64,1,128]{3,1,2,0:T(8,128)(2,1)S(1)} %collective-permute-done.1, bf16[1,64,64,128]{3,1,2,0:T(8,128)(2,1)S(1)} %get-tuple-element.26, bf16[1,64,64,128]{3,1,2,0:T(8,128)(2,1)S(1)} %get-tuple-element.27, bf16[4,64,64,128]{3,1,2,0:T(8,128)(2,1)} %copy-done.1, ...), kind=kLoop, calls=%fused_computation.17 | loop fusion | flops 52715520 | bytes 19768450 | tf_op jit(solution)/shard_map/convert_element_type | solution.py:162
  106.3 10.0 %fusion.2 = (f32[66,66,130]{2,0,1:T(8,128)}, f32[66,66,130]{2,0,1:T(8,128)S(1)}, f32[66,66,130]{2,0,1:T(8,128)S(1)}, f32[66,66,130]{2,0,1:T(8,128)}) fusion(f32[6,64,66,130]{3,1,2,0:T(8,128)} %fusion), kind=kLoop, calls=%fused_computation.24 | loop fusion | bytes 22239360 | tf_op jit(solution)/shard_map/squeeze | solution.py:59
  116.3 28.7 %fusion.45 = f32[64,64,128]{2,0,1:T(8,128)S(1)} fusion(f32[6,64,66,130]{3,1,2,0:T(8,128)} %fusion, f32[66,66,130]{2,0,1:T(8,128)S(1)} %get-tuple-element.18, f32[66,66,130]{2,0,1:T(8,128)S(1)} %get-tuple-element.17, f32[66,66,130]{2,0,1:T(8,128)} %get-tuple-element.19, bf16[64,64,128]{2,1,0:T(8,128)(2,1)S(1)} %copy-done.10), kind=kLoop, calls=%fused_computation.71 | loop fusion | flops 19922944 | bytes 62652416 | tf_op jit(solution)/shard_map/add | solution.py:68
  147.2 9.3 %convolution_bitcast_fusion = f32[512,64,64]{0,2,1:T(8,128)} fusion(f32[64,64,128]{2,0,1:T(8,128)S(1)} %fusion.139, f32[128,512]{1,0:T(8,128)S(1)} %copy-done), kind=kOutput, calls=%fused_computation.29 | convolution fusion | flops 3221225472 | bytes 10747904 | tf_op jit(solution)/shard_map/lar,rm->mla/dot_general | solution.py:29
  156.5 73.1 %reduce-scatter.2.cloned.1.call-done = f32[128,64,64]{0,2,1:T(8,128)} async-done(((f32[512,64,64]{0,2,1:T(8,128)}), f32[128,64,64]{0,2,1:T(8,128)}) %reduce-scatter.2.cloned.1.call-update) | async-done | bytes 2097168 | tf_op jit(solution)/shard_map/reduce_scatter | solution.py:140
  240.5 7.0 %all-to-all-start = ((f32[32,1,16384]{2,1,0:T(1,128)}), f32[32,1,16384]{2,1,0:T(1,128)S(1)}, u32[]{:S(2)}, u32[]{:S(2)}) async-start(f32[32,1,16384]{2,1,0:T(1,128)} %reshape.226), calls=%async_computation.1 | async-start | bytes 4194304 | tf_op jit(solution)/shard_map/all_to_all | solution.py:87
  248.7 26.2 %all-to-all-done = f32[32,1,16384]{2,1,0:T(1,128)S(1)} async-done(((f32[32,1,16384]{2,1,0:T(1,128)}), f32[32,1,16384]{2,1,0:T(1,128)S(1)}, u32[]{:S(2)}, u32[]{:S(2)}) %all-to-all-start) | async-done | bytes 2097184 | tf_op jit(solution)/shard_map/all_to_all | solution.py:87
  276.8 7.4 %reduce = f32[32,16384]{1,0:T(8,128)S(1)} reduce(f32[32,1,16384]{2,1,0:T(1,128)} %copy-done.8, f32[]{:T(128)} %broadcast.258), dimensions={1}, to_apply=%all_to_all.24.reduce_sub_computation | reduce | bytes 4194308 | tf_op jit(solution)/shard_map/all_to_all | solution.py:87
  287.2 6.7 %copy.48 = f32[4,64,32,64]{3,2,1,0:T(8,128)} copy(f32[4,64,32,64]{3,1,0,2:T(8,128)} %bitcast.206) | data formatting | bytes 4194304 | tf_op jit(solution)/shard_map/all_to_all | solution.py:87
  331.5 32.7 %all_to_all.33 = f32[32,1,16384]{2,1,0:T(1,128)} all-to-all(f32[32,1,16384]{2,1,0:T(1,128)S(1)} %reshape.228), channel_id=1, replica_groups=mesh['az'=32,'rad'=4] {'az'}, dimensions={0} | all-to-all | bytes 4194304 | tf_op jit(solution)/shard_map/all_to_all | solution.py:132
  364.2 7.4 %reduce.1 = f32[32,16384]{1,0:T(8,128)S(1)} reduce(f32[32,1,16384]{2,1,0:T(1,128)} %all_to_all.33, f32[]{:T(128)} %broadcast.258), dimensions={1}, to_apply=%all_to_all.27.reduce_sub_computation | reduce | bytes 4194308 | tf_op jit(solution)/shard_map/all_to_all | solution.py:132
  386.4 16.4 %multiply_bitcast_fusion.1 = (f32[64,64,128]{2,0,1:T(8,128)}, f32[1,64,64,128]{3,1,2,0:T(8,128)}, f32[1,64,64,128]{3,1,2,0:T(8,128)}, f32[1,64,64,128]{3,1,2,0:T...) fusion(f32[6,64,66,130]{3,1,2,0:T(8,128)} %fusion), kind=kLoop, calls=%fused_computation.171 | loop fusion | flops 6291456 | bytes 51118080 | tf_op jit(solution)/shard_map/div | solution.py:164
  402.8 17.0 %fusion.73 = f32[1,64,64,128]{3,1,2,0:T(8,128)} fusion(f32[66,66,130]{2,0,1:T(8,128)S(1)} %bitcast.203, f32[6,64,66,130]{3,1,2,0:T(8,128)} %fusion, f32[1,64,64,128]{3,1,2,0:T(8,128)} %get-tuple-element.15, f32[1,64,64,128]{3,1,2,0:T(8,128)} %get-tuple-element.14, f32[1,64,64,128]{3,1,2,0:T(8,128)} %get-tuple-element.13, ...), kind=kLoop, calls=%fused_computation.112 | loop fusion | flops 13631488 | bytes 55312384 | tf_op jit(solution)/shard_map/stack | solution.py:69
  419.8 19.6 %fusion.80 = f32[1,64,64,128]{3,1,2,0:T(8,128)} fusion(f32[66,66,130]{2,0,1:T(8,128)} %get-tuple-element.16, f32[6,64,66,130]{3,1,2,0:T(8,128)} %fusion, f32[1,64,64,128]{3,1,2,0:T(8,128)} %get-tuple-element.15, f32[1,64,64,128]{3,1,2,0:T(8,128)} %get-tuple-element.14, f32[1,64,64,128]{3,1,2,0:T(8,128)} %get-tuple-element.13, ...), kind=kLoop, calls=%fused_computation.124 | loop fusion | flops 13631488 | bytes 55312384 | tf_op jit(solution)/shard_map/stack | solution.py:69
  439.5 18.5 %fusion.87 = f32[1,64,64,128]{3,1,2,0:T(8,128)} fusion(f32[66,66,130]{2,0,1:T(8,128)} %get-tuple-element.16, f32[6,64,66,130]{3,1,2,0:T(8,128)} %fusion, f32[1,64,64,128]{3,1,2,0:T(8,128)} %get-tuple-element.15, f32[1,64,64,128]{3,1,2,0:T(8,128)} %get-tuple-element.14, f32[1,64,64,128]{3,1,2,0:T(8,128)} %get-tuple-element.13, ...), kind=kLoop, calls=%fused_computation.136 | loop fusion | flops 13631488 | bytes 55312384 | tf_op jit(solution)/shard_map/stack | solution.py:69
  464.7 10.2 %fusion.120 = f32[64,64,128]{2,0,1:T(8,128)S(1)} fusion(f32[512,64,64]{0,1,2:T(8,128)} %all-gather.2.cloned.1.call-done, f32[128,512]{1,0:T(8,128)S(1)} %copy-done), kind=kOutput, calls=%fused_computation.181 | convolution fusion | flops 3221225472 | bytes 10747904 | tf_op jit(solution)/shard_map/mla,rm->lar/dot_general | solution.py:29
  480.2 67.4 %all-reduce.1 = (f32[]{:T(128)}, f32[]{:T(128)}) all-reduce(f32[]{:T(128)} %fusion.1, f32[]{:T(128)S(6)} %add.401), channel_id=1, replica_groups=mesh['az'=32,'rad'=4] {'az'}, use_global_device_ids=true, to_apply=%region_1.2 | all-reduce | flops 2 | bytes 16 | tf_op jit(solution)/shard_map/psum | solution.py:168
  547.6 23.0 %all-reduce.2 = (f32[]{:T(128)}, f32[]{:T(128)}) all-reduce(f32[]{:T(128)} %get-tuple-element.5, f32[]{:T(128)} %get-tuple-element.6), channel_id=1, replica_groups=mesh['az'=32,'rad'=4] {'rad'}, use_global_device_ids=true, to_apply=%region_2.3 | all-reduce | flops 2 | bytes 16 | tf_op jit(solution)/shard_map/psum | solution.py:168
  (85 shorter events, 115.4 us)
Async XLA Ops:
  6.5 140.6 %copy-start = (f32[128,512]{1,0:T(8,128)S(1)}, f32[128,512]{1,0:T(8,128)}, u32[]{:S(2)}) copy-start(f32[128,512]{1,0:T(8,128)} %param.10) | copy-start | bytes 786436
  6.5 5.1 copy-start.11
  6.5 223.0 %reduce-scatter.2.cloned.1.call-start = ((), (), s32[]{:S(2)}) async-start(), calls=%async_computation.3 | async-start | bytes 10485760 | tf_op jit(solution)/shard_map/reduce_scatter | solution.py:140
  6.5 5.1 copy-start.12
  11.6 2.0 copy-start.1
  13.7 9.5 %collective-permute-start.1 = (bf16[6,64,1,128]{3,1,2,0:T(8,128)(2,1)S(1)}, bf16[6,64,1,128]{3,1,2,0:T(8,128)(2,1)S(1)}, u32[]{:S(2)}, u32[]{:S(2)}) collective-permute-start(bf16[6,64,1,128]{3,1,2,0:T(8,128)(2,1)S(1)} %get-tuple-element.23), channel_id=1, source_target_pairs={{4,0},{8,4},{12,8},{16,12},{20,16},{24,20},{28,24},{32,28},{36,32}... | collective-permute-start | bytes 294920 | tf_op jit(solution)/shard_map/ppermute | solution.py:21
  21.5 7.7 %collective-permute-start = (bf16[6,64,1,128]{3,1,2,0:T(8,128)(2,1)S(1)}, bf16[6,64,1,128]{3,1,2,0:T(8,128)(2,1)S(1)}, u32[]{:S(2)}, u32[]{:S(2)}) collective-permute-start(bf16[6,64,1,128]{3,1,2,0:T(8,128)(2,1)S(1)} %get-tuple-element.22), channel_id=1, source_target_pairs={{0,4},{4,8},{8,12},{12,16},{16,20},{20,24},{24,28},{28,32},{32,36}... | collective-permute-start | bytes 294920 | tf_op jit(solution)/shard_map/ppermute | solution.py:19
  47.9 13.4 %collective-permute-start.3 = (bf16[6,64,66,1]{2,1,3,0:T(8,128)(2,1)S(1)}, bf16[6,64,66,1]{2,1,3,0:T(8,128)(2,1)S(1)}, u32[]{:S(2)}, u32[]{:S(2)}) collective-permute-start(bf16[6,64,66,1]{2,1,3,0:T(8,128)(2,1)S(1)} %copy.41), channel_id=1, source_target_pairs={{1,0},{2,1},{3,2},{0,3},{5,4},{6,5},{7,6},{4,7},{9,8},{10,9},{11,1... | collective-permute-start | bytes 152072 | tf_op jit(solution)/shard_map/ppermute | solution.py:21
  58.5 14.2 %collective-permute-start.2 = (bf16[6,64,66,1]{2,1,3,0:T(8,128)(2,1)S(1)}, bf16[6,64,66,1]{2,1,3,0:T(8,128)(2,1)S(1)}, u32[]{:S(2)}, u32[]{:S(2)}) collective-permute-start(bf16[6,64,66,1]{2,1,3,0:T(8,128)(2,1)S(1)} %copy.40), channel_id=1, source_target_pairs={{0,1},{1,2},{2,3},{3,0},{4,5},{5,6},{6,7},{7,4},{8,9},{9,10},{10,1... | collective-permute-start | bytes 152072 | tf_op jit(solution)/shard_map/ppermute | solution.py:19
  106.3 10.0 %copy-start.10 = (bf16[64,64,128]{2,1,0:T(8,128)(2,1)S(1)}, bf16[64,64,128]{2,1,0:T(8,128)(2,1)}, u32[]{:S(2)}) copy-start(bf16[64,64,128]{2,1,0:T(8,128)(2,1)} %param.7) | copy-start | bytes 3145732
  145.0 2.1 copy-start.2
  240.5 34.5 %all-to-all-start = ((f32[32,1,16384]{2,1,0:T(1,128)}), f32[32,1,16384]{2,1,0:T(1,128)S(1)}, u32[]{:S(2)}, u32[]{:S(2)}) async-start(f32[32,1,16384]{2,1,0:T(1,128)} %reshape.226), calls=%async_computation.1 | async-start | bytes 4194304 | tf_op jit(solution)/shard_map/all_to_all | solution.py:87
  247.5 217.2 %all-gather.2.cloned.1.call-start = ((), (), s32[]{:S(2)}) async-start(), calls=%async_computation.4 | async-start | bytes 10485760 | tf_op jit(solution)/shard_map/all_gather | solution.py:148
  275.0 1.3 copy-start.8
  386.4 16.4 %slice-start = ((s8[4866048]{0:T(1024)(128)(4,1)}), s8[671744]{0:T(1024)(128)(4,1)S(1)}, s32[]{:S(2)}) async-start(s8[4866048]{0:T(1024)(128)(4,1)} %bitcast.202), calls=%async_computation.5 | async-start | bytes 1343488
  386.4 16.4 %slice-start.1 = ((s8[4866048]{0:T(1024)(128)(4,1)}), s8[4194304]{0:T(1024)(128)(4,1)S(1)}, s32[]{:S(2)}) async-start(s8[4866048]{0:T(1024)(128)(4,1)} %bitcast.202), calls=%async_computation.6 | async-start | bytes 8388608
  439.4 18.5 %copy-start.3 = (f32[64,64,128]{2,0,1:T(8,128)S(1)}, f32[64,64,128]{2,0,1:T(8,128)}, u32[]{:S(2)}) copy-start(f32[64,64,128]{2,0,1:T(8,128)} %copy-done.2) | copy-start | bytes 6291460
  439.4 18.5 %copy-start.4 = (f32[1,64,64,128]{3,1,2,0:T(8,128)S(1)}, f32[1,64,64,128]{3,1,2,0:T(8,128)}, u32[]{:S(2)}) copy-start(f32[1,64,64,128]{3,1,2,0:T(8,128)} %fusion.73) | copy-start | bytes 6291460
  457.9 4.5 copy-start.5
  458.0 4.5 copy-start.6
  458.0 4.5 copy-start.7
  571.8 4.2 copy-start.9
Sparse Core Ops, SparseCore 0:
  156.6 72.8 reduce-scatter.1
  386.5 64.0 all-gather.1
